TPU v7x, 128 devices: a whole 4x4x4 slice. The times are simulated.
128 devices in a mesh: row: 16 (over x, z_hi, core), col: 8 (over y, z_lo).
Axes of the slice: x: 4, y: 4, z: 4 (z_hi: 2, z_lo: 2; z = z_hi * 2 + z_lo), core: 2. Of those that a mesh axis runs over, the one named last changes fastest.
Arguments:
- tile_values: bfloat16 [256, 8, 4, 128, 128], P(('row', 'col')), may hold values from 0 to 1
- tile_columns: int32 [256, 8, 4], P(('row', 'col')), may hold values from -1 to 255, as said below
- owner_map: int32 [256], replicated, may hold values from 0 to 255, as said below
- section_rows: int32 [2], replicated, may hold values from 0 to 15, as said below
Outputs:
- inflated: bfloat16 [32768, 12288], P('row', 'col')
Inputs may be any that keep to these rules, and one draw needn't show every extreme that they name: `tile_columns`: in each tile row and block-column b, the first 1 to 4 slots name distinct tile columns within b * 32 to b * 32 + 31 and the remaining slots hold -1; some tile row uses all 4 slots. A permutation of the tile rows; of the tile rows t in each aligned group of 16, exactly 1 have owner_map[t] in each block-row's range of 16 positions. `section_rows`: distinct block-rows; the last block-row is always one of them.
All inputs are finite; a program needn't handle non-finite values.
Results may differ from a plain program's by a relative error of at most 0.001.
Values may be sent and summed in bfloat16 or wider, within the bound.
A program may use at most 128 MiB of HBM per device.

v0:
```python
import jax
import jax.numpy as jnp
from jax import lax
from jax.sharding import Mesh
from jax.sharding import PartitionSpec as P

TILE = 128
SLAB = 12
SECTIONS = 2
ROW = ("row_0", "row_1", "row_2")
ROW_COL = ("row_0", "row_1", "row_2", "col")


def cut_along(x, dim, peers):
    dims = x.shape
    tiles = x.reshape(*dims[:dim], peers, dims[dim] // peers, *dims[dim + 1 :])
    return jnp.moveaxis(tiles, dim, 0)


def joined_along(tiles, dim):
    dims = list(tiles.shape[1:])
    dims[dim] *= tiles.shape[0]
    return jnp.moveaxis(tiles, 0, dim).reshape(dims)


def moved_by_axis(tiles, axes, turns):
    inside = tiles.shape[1:]
    out = tiles.reshape(*(lax.axis_size(a) for a in axes), *inside)
    for k in turns:
        out = lax.all_to_all(out, axes[k], k, k, tiled=True)
    return out.reshape(-1, *inside)


def two_step_exchange(x, groups, turns, split_dim, concat_dim):
    peers = lax.axis_size(groups[0]) * lax.axis_size(groups[1])
    tiles = cut_along(x, split_dim, peers)
    return joined_along(moved_by_axis(tiles, groups, turns), concat_dim)


def broadcast(x, axis, root):
    mine = lax.axis_index(axis) == root
    return lax.psum(jnp.where(mine, x, jnp.zeros_like(x)), axis)


def copy_for_each(x, axis):
    peers = lax.axis_size(axis)
    return lax.all_to_all(jnp.broadcast_to(x[None], (peers, *x.shape)), axis, 0, 0, tiled=True)


def over_copies(x, axis):
    return copy_for_each(x, axis).sum(axis=0)


def densify(values_in, columns_in, first_col):
    relative = columns_in - first_col
    picker = (relative[..., None] == jnp.arange(SLAB, dtype=jnp.int32)).astype(jnp.bfloat16)
    spread = jnp.einsum("nkab,nkj->najb", values_in, picker, preferred_element_type=jnp.float32)
    return spread.astype(jnp.bfloat16).reshape(values_in.shape[0], TILE, SLAB * TILE)


def per_device(tile_values, tile_columns, owner_map, section_rows):
    n_row = lax.axis_size(ROW)
    n_col = lax.axis_size("col")
    row_id = lax.axis_index(ROW)
    col_id = lax.axis_index("col")
    tile_count = owner_map.shape[0]
    rows_block = tile_values.shape[0] * n_col
    cols_block = tile_values.shape[0] * n_row
    first_col = col_id * cols_block
    every_columns = lax.all_gather(tile_columns, ROW_COL, axis=0, tiled=True)
    every_tile = jnp.arange(tile_count, dtype=jnp.int32)
    inverse = jnp.zeros((tile_count,), jnp.int32).at[owner_map].set(every_tile)
    grid_columns = every_columns[inverse]

    def block_lists(block_row, block_col):
        rows_part = lax.dynamic_slice_in_dim(grid_columns, block_row * rows_block, rows_block, 0)
        return jnp.take(rows_part, block_col, axis=1)

    spread_vals = lax.all_to_all(tile_values, "col", split_axis=1, concat_axis=0, tiled=True)
    spread_vals = spread_vals[:, 0]
    local_rows = jnp.arange(rows_block, dtype=jnp.int32)
    source_tiles = row_id * rows_block + local_rows
    target_block = owner_map[source_tiles] // rows_block
    send_order = jnp.argsort(target_block * rows_block + local_rows)
    recv_vals = two_step_exchange(
        spread_vals[send_order], (("row_0", "row_1"), "row_2"), (1, 0), 0, 0
    )
    owned = owner_map // rows_block == row_id
    arrived = jnp.argsort(jnp.where(owned, every_tile, every_tile + tile_count))[:rows_block]
    new_local = owner_map[arrived] - row_id * rows_block
    placed = jnp.argsort(new_local)
    block_vals = recv_vals[placed]
    slot_values = []
    slot_targets = []
    panels = []
    for section in range(SECTIONS):
        section_row = section_rows[section]
        source_col = section_row * n_col // n_row
        panel_vals = broadcast(block_vals, "col", source_col)
        panel_cols = block_lists(row_id, source_col)
        list_vals = broadcast(block_vals, ROW, section_row)
        panel_dense = densify(list_vals, block_lists(section_row, col_id), first_col)
        relative = panel_cols - section_row * rows_block
        inside = (relative >= 0) & (relative < rows_block)
        slot_targets.append(jnp.where(inside, relative, 0) + section * rows_block)
        slot_values.append(panel_vals * inside[..., None, None].astype(jnp.bfloat16))
        panels.append(panel_dense)
    all_values = jnp.concatenate(slot_values, axis=1)
    all_targets = jnp.concatenate(slot_targets, axis=1)
    all_panels = jnp.concatenate(panels, axis=0).reshape(SECTIONS * rows_block * TILE, SLAB * TILE)
    inner_count = SECTIONS * rows_block
    left_picker = (all_targets[..., None] == jnp.arange(inner_count, dtype=jnp.int32)).astype(
        jnp.bfloat16
    )
    left_dense = jnp.einsum(
        "nkab,nkj->najb", all_values, left_picker, preferred_element_type=jnp.float32
    )
    left_dense = left_dense.astype(jnp.bfloat16).reshape(rows_block * TILE, inner_count * TILE)
    expanded = jnp.dot(left_dense, all_panels, preferred_element_type=jnp.float32)
    squares = expanded * expanded
    column_part = jnp.sum(squares, axis=0)
    column_total = over_copies(column_part, ROW)
    factor = tile_count * TILE / (column_total + 1e-06)
    return (squares * factor).astype(jnp.bfloat16)


def solution(mesh):
    split = Mesh(
        mesh.devices.reshape(4, 2, 2, mesh.shape["col"]), ("row_0", "row_1", "row_2", "col")
    )
    in_specs = (P(ROW_COL, None, None, None, None), P(ROW_COL, None, None), P(), P())
    out_specs = P(ROW, "col")
    return jax.shard_map(
        per_device, mesh=split, in_specs=in_specs, out_specs=out_specs, check_vma=False
    )
```

profile of v0, /device:TPU:1, one launch (start us, length us, event | category | flops | bytes accessed | tf_op | source)
XLA Modules:
  0.0 567.8 jit_solution(13753688839111758612)
XLA Ops:
  6.5 3.2 copy.88
  9.7 6.5 %all-to-all-start = ((bf16[2,8,4,128,128]{4,3,2,0,1:T(8,128)(2,1)}), bf16[2,8,4,128,128]{4,3,2,0,1:T(8,128)(2,1)S(1)}, u32[]{:S(2)}, u32[]{:S(2)}) async-start(bf16[2,8,4,128,128]{4,3,2,0,1:T(8,128)(2,1)} %copy.88), calls=%async_computation | async-start | bytes 4194304 | tf_op jit(solution)/shard_map/all_to_all | solution.py:79
  16.2 0.7 gather_fusion.1
  16.9 3.2 sort.49
  20.1 1.3 sort.48
  21.5 25.3 %all-to-all-done = bf16[2,8,4,128,128]{4,3,2,0,1:T(8,128)(2,1)S(1)} async-done(((bf16[2,8,4,128,128]{4,3,2,0,1:T(8,128)(2,1)}), bf16[2,8,4,128,128]{4,3,2,0,1:T(8,128)(2,1)S(1)}, u32[]{:S(2)}, u32[]{:S(2)}) %all-to-all-start) | async-done | bytes 2097184 | tf_op jit(solution)/shard_map/all_to_all | solution.py:79
  46.8 2.1 gather_fusion.2
  48.9 1.7 copy.89
  50.7 6.6 %all_to_all.31 = bf16[8,2,1,4,128,128]{5,4,3,0,2,1:T(8,128)(2,1)S(1)} all-to-all(bf16[8,2,1,4,128,128]{5,4,3,0,2,1:T(8,128)(2,1)S(1)} %copy.89), channel_id=1, replica_groups=mesh['row_0'=4,'row_1'=2,'row_2'=2,'col'=8] {'row_2'}, dimensions={1} | all-to-all | bytes 4194304 | tf_op jit(solution)/shard_map/all_to_all | solution.py:30
  57.3 1.5 copy.90
  58.7 7.2 %all-to-all-start.2 = ((bf16[8,2,1,4,128,128]{5,4,3,1,2,0:T(8,128)(2,1)}), bf16[8,2,1,4,128,128]{5,4,3,1,2,0:T(8,128)(2,1)S(1)}, u32[]{:S(2)}, u32[]{:S(2)}) async-start(bf16[8,2,1,4,128,128]{5,4,3,1,2,0:T(8,128)(2,1)} %copy.90), calls=%async_computation.2 | async-start | bytes 4194304 | tf_op jit(solution)/shard_map/all_to_all | solution.py:30
  65.9 0.0 all-reduce.5.cloned.1.call-start
  66.0 0.6 fusion.22
  69.1 0.7 gather_fusion.3
  69.8 1.3 sort.50
  71.1 25.7 %all-to-all-done.2 = bf16[8,2,1,4,128,128]{5,4,3,1,2,0:T(8,128)(2,1)S(1)} async-done(((bf16[8,2,1,4,128,128]{5,4,3,1,2,0:T(8,128)(2,1)}), bf16[8,2,1,4,128,128]{5,4,3,1,2,0:T(8,128)(2,1)S(1)}, u32[]{:S(2)}, u32[]{:S(2)}) %all-to-all-start.2) | async-done | bytes 2097184 | tf_op jit(solution)/shard_map/all_to_all | solution.py:30
  96.8 2.1 gather_fusion.4
  99.0 7.6 %broadcast_select_fusion.3 = (bf16[16,4,128,128]{3,1,2,0:T(4,128)(2,1)}, bf16[16,4,128,128]{3,1,2,0:T(4,128)(2,1)}, bf16[16,4,128,128]{3,1,2,0:T(4,128)(2,1)}, bf16[16,4,128,128]{3,1,2,0:T(4,128)(2,1)}) fusion(pred[]{:T(512)S(6)} %eq.60, bf16[16,4,128,128]{3,2,1,0:T(8,128)(2,1)} %gather_fusion.4, pred[]{:T(512)S(6)} %eq.63, pred[]{:T(512)S(6)} %eq.67, ...), kind=kLoop, calls=%fused_computation.21 | loop fusion | flops 4194304 | bytes 10485764 | tf_op jit(solution)/shard_map/jit(_where)/select_n | solution.py:42
  106.6 0.0 all-reduce.5.cloned.1.call-update
  106.6 0.0 all-reduce.7.cloned.1.call-start
  106.7 0.7 all-reduce.7.cloned.1.call-update
  108.7 1.4 scatter_custom_fusion
  110.1 301.1 %all_gather.3 = s32[256,8,4]{1,2,0:T(4,128)S(1)} all-gather(s32[2,8,4]{1,2,0:T(4,128)S(1)} %copy-done.3), channel_id=1, replica_groups=mesh['row_0'=4,'row_1'=2,'row_2'=2,'col'=8] {'row_0','row_1','row_2','col'}, dimensions={0}, use_global_device_ids=true | all-gather | bytes 33024 | tf_op jit(solution)/shard_map/all_gather | solution.py:70
  411.2 1.0 gather_fusion
  412.2 0.1 dynamic-slice_select_fusion.3
  412.3 0.1 copy.85
  412.4 0.1 copy.86
  412.5 0.1 copy.95
  412.6 0.1 copy.99
  412.8 0.1 copy.94
  412.9 0.1 copy.92
  413.0 0.1 copy.87
  413.1 0.1 copy.100
  413.2 0.1 copy.96
  413.2 7.1 %convert_bitcast_fusion = bf16[16,128,12,128]{3,2,1,0:T(8,128)(2,1)} fusion(bf16[16,4,128,128]{3,1,2,0:T(4,128)(2,1)} %get-tuple-element.23, s32[16,4]{1,0:T(8,128)S(1)} %copy.100), kind=kOutput, calls=%fused_computation.13 | convolution fusion | flops 28312320 | bytes 8388864 | tf_op jit(solution)/shard_map/nkab,nkj->najb/dot_general | solution.py:57
  420.4 12.2 %copy.102 = bf16[16,128,12,128]{1,3,2,0:T(8,128)(2,1)} copy(bf16[16,128,12,128]{3,2,1,0:T(8,128)(2,1)} %convert_bitcast_fusion) | data formatting | bytes 12582912 | tf_op jit(solution)/shard_map/convert_element_type | solution.py:58
  432.6 6.4 %convert_bitcast_fusion.1 = bf16[16,128,12,128]{3,2,1,0:T(8,128)(2,1)} fusion(bf16[16,4,128,128]{3,1,2,0:T(4,128)(2,1)S(1)} %copy-done.1, s32[16,4]{1,0:T(8,128)S(1)} %copy.96), kind=kOutput, calls=%fused_computation.14 | convolution fusion | flops 28312320 | bytes 8388864 | tf_op jit(solution)/shard_map/nkab,nkj->najb/dot_general | solution.py:57
  439.0 12.0 %copy.98 = bf16[16,128,12,128]{1,3,2,0:T(8,128)(2,1)} copy(bf16[16,128,12,128]{3,2,1,0:T(8,128)(2,1)} %convert_bitcast_fusion.1) | data formatting | bytes 12582912 | tf_op jit(solution)/shard_map/convert_element_type | solution.py:58
  451.0 10.5 %pad_maximum_fusion = bf16[32,128,1536]{1,2,0:T(8,128)(2,1)} fusion(bf16[16,128,1536]{1,2,0:T(8,128)(2,1)} %bitcast.70, bf16[16,128,1536]{1,2,0:T(8,128)(2,1)} %bitcast.71), kind=kLoop, calls=%fused_computation.9 | loop fusion | flops 6291456 | bytes 25165824 | tf_op jit(solution)/shard_map/concatenate | solution.py:110
  461.5 16.6 %copy.103 = bf16[32,128,1536]{2,1,0:T(8,128)(2,1)} copy(bf16[32,128,1536]{1,2,0:T(8,128)(2,1)} %pad_maximum_fusion) | data formatting | bytes 25165824 | tf_op jit(solution)/shard_map/concatenate | solution.py:110
  478.1 4.0 broadcast_multiply_fusion
  482.1 2.3 broadcast_multiply_fusion.1
  484.4 9.9 %convolution_convert_fusion = bf16[16,32,128,128]{3,1,2,0:T(8,128)(2,1)} fusion(bf16[16,4,128,128]{3,1,2,0:T(4,128)(2,1)} %broadcast_multiply_fusion, bf16[16,4,128,128]{3,1,2,0:T(4,128)(2,1)} %broadcast_multiply_fusion.1, s32[16,8]{1,0:T(8,128)S(1)} %copy.87), kind=kOutput, calls=%fused_computation.12 | convolution fusion | flops 150999040 | bytes 20972032 | tf_op jit(solution)/shard_map/nkab,nkj->najb/dot_general | solution.py:115
  494.3 31.4 %multiply_reduce_fusion = (f32[1536]{0:T(1024)S(1)}, f32[2048,1536]{1,0:T(8,128)}) fusion(bf16[4096,1536]{1,0:T(8,128)(2,1)S(1)} %bitcast.74, bf16[256,8,32,128]{3,2,1,0:T(8,128)(2,1)} %bitcast.69), kind=kOutput, calls=%fused_computation.11 | convolution fusion | flops 25776093184 | bytes 41949184 | tf_op jit(solution)/shard_map/dot_general | solution.py:119
  525.7 0.1 broadcast_in_dim.48
  525.8 26.1 %all_to_all.32 = f32[16,1,1536]{2,1,0:T(1,128)S(1)} all-to-all(f32[16,1,1536]{2,1,0:T(1,128)S(1)} %broadcast_in_dim.48), channel_id=1, replica_groups=mesh['row_0'=4,'row_1'=2,'row_2'=2,'col'=8] {'row_0','row_1','row_2'}, dimensions={0} | all-to-all | bytes 196608 | tf_op jit(solution)/shard_map/all_to_all | solution.py:47
  551.8 0.1 reduce_sum.19
  551.9 9.0 %multiply_convert_fusion = bf16[2048,1536]{1,0:T(8,128)(2,1)} fusion(f32[2048,1536]{1,0:T(8,128)} %get-tuple-element.40, f32[1536]{0:T(1024)S(1)} %add_divide_fusion), kind=kLoop, calls=%fused_computation.10 | loop fusion | flops 9437184 | bytes 18880512 | tf_op jit(solution)/shard_map/convert_element_type | solution.py:124
  (41 shorter events, 0.2 us)
Async XLA Ops:
  9.7 6.5 %copy-start = (s32[256]{0:T(256)S(1)}, s32[256]{0:T(256)}, u32[]{:S(2)}) copy-start(s32[256]{0:T(256)} %param.8) | copy-start | bytes 3076
  9.7 37.1 %all-to-all-start = ((bf16[2,8,4,128,128]{4,3,2,0,1:T(8,128)(2,1)}), bf16[2,8,4,128,128]{4,3,2,0,1:T(8,128)(2,1)S(1)}, u32[]{:S(2)}, u32[]{:S(2)}) async-start(bf16[2,8,4,128,128]{4,3,2,0,1:T(8,128)(2,1)} %copy.88), calls=%async_computation | async-start | bytes 4194304 | tf_op jit(solution)/shard_map/all_to_all | solution.py:79
  58.7 7.2 %copy-start.4 = (s32[2]{0:T(128)S(1)}, s32[2]{0:T(128)}, u32[]{:S(2)}) copy-start(s32[2]{0:T(128)} %param.9) | copy-start | bytes 28
  58.7 38.1 %all-to-all-start.2 = ((bf16[8,2,1,4,128,128]{5,4,3,1,2,0:T(8,128)(2,1)}), bf16[8,2,1,4,128,128]{5,4,3,1,2,0:T(8,128)(2,1)S(1)}, u32[]{:S(2)}, u32[]{:S(2)}) async-start(bf16[8,2,1,4,128,128]{5,4,3,1,2,0:T(8,128)(2,1)} %copy.90), calls=%async_computation.2 | async-start | bytes 4194304 | tf_op jit(solution)/shard_map/all_to_all | solution.py:30
  65.9 347.3 %all-reduce.5.cloned.1.call-start = ((), (), s32[]{:S(2)}) async-start(), calls=%async_computation.4 | async-start | bytes 8388608 | tf_op jit(solution)/shard_map/psum | solution.py:42
  106.6 371.5 %all-reduce.7.cloned.1.call-start = ((), (), s32[]{:S(2)}) async-start(), calls=%async_computation.5 | async-start | bytes 8388608 | tf_op jit(solution)/shard_map/psum | solution.py:42
  106.7 3.4 copy-start.3
  420.3 12.2 %copy-start.1 = (bf16[16,4,128,128]{3,1,2,0:T(4,128)(2,1)S(1)}, bf16[16,4,128,128]{3,1,2,0:T(4,128)(2,1)}, u32[]{:S(2)}) copy-start(bf16[16,4,128,128]{3,1,2,0:T(4,128)(2,1)} %get-tuple-element.24) | copy-start | bytes 6291460
  478.1 4.0 copy-start.2
  482.1 12.2 %slice-start = ((s8[12582912]{0:T(1024)(128)(4,1)}), s8[4194304]{0:T(1024)(128)(4,1)S(1)}, s32[]{:S(2)}) async-start(s8[12582912]{0:T(1024)(128)(4,1)} %bitcast.72), calls=%async_computation.6 | async-start | bytes 8388608
  484.4 9.9 %slice-start.1 = ((s8[12582912]{0:T(1024)(128)(4,1)}), s8[4194304]{0:T(1024)(128)(4,1)S(1)}, s32[]{:S(2)}) async-start(s8[12582912]{0:T(1024)(128)(4,1)} %bitcast.72), calls=%async_computation.7 | async-start | bytes 8388608
  484.4 9.9 %slice-start.2 = ((s8[12582912]{0:T(1024)(128)(4,1)}), s8[4194304]{0:T(1024)(128)(4,1)S(1)}, s32[]{:S(2)}) async-start(s8[12582912]{0:T(1024)(128)(4,1)} %bitcast.72), calls=%async_computation.8 | async-start | bytes 8388608
Sparse Core Ops, SparseCore 0:
  106.7 147.2 all-reduce.4
  256.6 187.8 all-reduce.6
where the time goes:
time: 569 us; the launch traced here: 568 us
  blocking collectives  334 us (59%)
  local copies, waits for them, and re-layouts  56.7 us (10%)
  matrix products  54.8 us (10%)
  waiting for transfers between devices  51.8 us (9%)
  other arithmetic  39.6 us (7%)
  between operations  17.4 us (3%)
  starting transfers between devices  13.7 us (2%)
    all_gather x1, blocking collectives, per_device(): every_columns = lax.all_gather(tile_columns, ROW_COL, axis=0, tiled=True)  301 us
    dot_general x1, matrix products, per_device(): jnp.dot(left_dense, all_panels, preferred_element_type=jnp.float32)  31.4 us
    all_to_all x1, blocking collectives, copy_for_each(): lax.all_to_all(jnp.broadcast_to(x[None], (peers, *x.shape)), axis, 0, 0,...  26.1 us
    all_to_all x1, waiting for transfers between devices, moved_by_axis(): out = lax.all_to_all(out, axes[k], k, k, tiled=True)  25.7 us
    all_to_all x1, waiting for transfers between devices, per_device(): lax.all_to_all(tile_values, 'col', split_axis=1, concat_axis=0, tiled=True)  25.3 us
    convert_element_type x2, local copies, waits for them, and re-layouts, densify(): spread.astype(jnp.bfloat16).reshape(values_in.shape[0], TILE, SLAB * TILE)  24.2 us
    concatenate x1, local copies, waits for them, and re-layouts, per_device(): jnp.concatenate(panels, axis=0)  16.6 us
    dot_general x2, matrix products, densify(): jnp.einsum('nkab,nkj->najb', values_in, picker, preferred_element_type=jn...  13.5 us
  transfers between devices with their start and end apart: 4, of which 2 were waited for; matrix products, arithmetic and copies ran while one was open for 13% of the time, Pallas kernels for 0%

commit v1 on v0

--- a/solution.py
+++ b/solution.py
@@ -67,7 +67,9 @@
     rows_block = tile_values.shape[0] * n_col
     cols_block = tile_values.shape[0] * n_row
     first_col = col_id * cols_block
-    every_columns = lax.all_gather(tile_columns, ROW_COL, axis=0, tiled=True)
+    every_columns = jnp.concatenate(
+        lax.all_to_all(jnp.stack([tile_columns] * lax.axis_size(ROW_COL)), ROW_COL, 0, 0), axis=0
+    )
     every_tile = jnp.arange(tile_count, dtype=jnp.int32)
     inverse = jnp.zeros((tile_count,), jnp.int32).at[owner_map].set(every_tile)
     grid_columns = every_columns[inverse]

time: 569 us -> 525 us (0.923)
  blocking collectives: 334 us -> 21.2 us
  waiting for transfers between devices: 51.8 us -> 314 us
    all_gather x1 -> x0, blocking collectives: 301 us -> none  [per_device(): every_columns = lax.all_gather(tile_columns, ROW_COL, axis=0, tiled=True)]
    psum x2, waiting for transfers between devices: 0.01 us -> 250 us  [broadcast(): return lax.psum(jnp.where(mine, x, jnp.zeros_like(x)), axis)]
    all_to_all x0 -> x1, waiting for transfers between devices: none -> 12.2 us  [per_device(): lax.all_to_all(jnp.stack([tile_columns] * lax.axis_size(ROW_COL)), ROW_CO...]
    all_to_all x1, blocking collectives: 26.1 us -> 14.6 us  [copy_for_each(): lax.all_to_all(jnp.broadcast_to(x[None], (peers, *x.shape)), axis, 0, 0,...]
  transfers between devices with their start and end apart: 4 -> 5, of which waited for: 2 -> 5; matrix products, arithmetic and copies ran while one was open for 13% -> 15% of each run, Pallas kernels for 0% -> 0%
where the time goes in v1:
time: 525 us; the launch traced here: 524 us
  waiting for transfers between devices  314 us (60%)
  local copies, waits for them, and re-layouts  57.8 us (11%)
  matrix products  54.8 us (10%)
  other arithmetic  39.7 us (8%)
  blocking collectives  21.2 us (4%)
  starting transfers between devices  18.6 us (4%)
  between operations  17.4 us (3%)
    psum x2, waiting for transfers between devices, broadcast(): return lax.psum(jnp.where(mine, x, jnp.zeros_like(x)), axis)  250 us
    dot_general x1, matrix products, per_device(): jnp.dot(left_dense, all_panels, preferred_element_type=jnp.float32)  31.4 us
    all_to_all x1, waiting for transfers between devices, moved_by_axis(): out = lax.all_to_all(out, axes[k], k, k, tiled=True)  25.7 us
    all_to_all x1, waiting for transfers between devices, per_device(): lax.all_to_all(tile_values, 'col', split_axis=1, concat_axis=0, tiled=True)  25.3 us
    convert_element_type x2, local copies, waits for them, and re-layouts, densify(): spread.astype(jnp.bfloat16).reshape(values_in.shape[0], TILE, SLAB * TILE)  24.2 us
    concatenate x1, local copies, waits for them, and re-layouts, per_device(): jnp.concatenate(panels, axis=0)  16.7 us
    all_to_all x1, blocking collectives, copy_for_each(): lax.all_to_all(jnp.broadcast_to(x[None], (peers, *x.shape)), axis, 0, 0,...  14.6 us
    dot_general x2, matrix products, densify(): jnp.einsum('nkab,nkj->najb', values_in, picker, preferred_element_type=jn...  13.5 us
  transfers between devices with their start and end apart: 5, of which 5 were waited for; matrix products, arithmetic and copies ran while one was open for 15% of the time, Pallas kernels for 0%

profile of v1, /device:TPU:1, one launch (start us, length us, event | category | flops | bytes accessed | tf_op | source)
XLA Modules:
  0.0 523.6 jit_solution(7952647315136389395)
XLA Ops:
  6.5 3.2 copy.85
  9.7 6.5 %all-to-all-start.1 = ((bf16[2,8,4,128,128]{4,3,2,0,1:T(8,128)(2,1)}), bf16[2,8,4,128,128]{4,3,2,0,1:T(8,128)(2,1)S(1)}, u32[]{:S(2)}, u32[]{:S(2)}) async-start(bf16[2,8,4,128,128]{4,3,2,0,1:T(8,128)(2,1)} %copy.85), calls=%async_computation.1 | async-start | bytes 4194304 | tf_op jit(solution)/shard_map/all_to_all | solution.py:81
  16.2 0.7 gather_fusion.1
  16.9 3.2 sort.49
  20.1 1.3 sort.48
  21.5 25.3 %all-to-all-done.1 = bf16[2,8,4,128,128]{4,3,2,0,1:T(8,128)(2,1)S(1)} async-done(((bf16[2,8,4,128,128]{4,3,2,0,1:T(8,128)(2,1)}), bf16[2,8,4,128,128]{4,3,2,0,1:T(8,128)(2,1)S(1)}, u32[]{:S(2)}, u32[]{:S(2)}) %all-to-all-start.1) | async-done | bytes 2097184 | tf_op jit(solution)/shard_map/all_to_all | solution.py:81
  46.8 2.1 gather_fusion.2
  48.9 1.7 copy.86
  50.7 6.6 %all_to_all.36 = bf16[8,2,1,4,128,128]{5,4,3,0,2,1:T(8,128)(2,1)S(1)} all-to-all(bf16[8,2,1,4,128,128]{5,4,3,0,2,1:T(8,128)(2,1)S(1)} %copy.86), channel_id=1, replica_groups=mesh['row_0'=4,'row_1'=2,'row_2'=2,'col'=8] {'row_2'}, dimensions={1} | all-to-all | bytes 4194304 | tf_op jit(solution)/shard_map/all_to_all | solution.py:30
  57.3 1.5 copy.87
  58.7 7.2 %all-to-all-start.3 = ((bf16[8,2,1,4,128,128]{5,4,3,1,2,0:T(8,128)(2,1)}), bf16[8,2,1,4,128,128]{5,4,3,1,2,0:T(8,128)(2,1)S(1)}, u32[]{:S(2)}, u32[]{:S(2)}) async-start(bf16[8,2,1,4,128,128]{5,4,3,1,2,0:T(8,128)(2,1)} %copy.87), calls=%async_computation.3 | async-start | bytes 4194304 | tf_op jit(solution)/shard_map/all_to_all | solution.py:30
  66.0 0.6 fusion.22
  69.1 0.7 gather_fusion.3
  69.8 1.3 sort.50
  71.1 25.7 %all-to-all-done.3 = bf16[8,2,1,4,128,128]{5,4,3,1,2,0:T(8,128)(2,1)S(1)} async-done(((bf16[8,2,1,4,128,128]{5,4,3,1,2,0:T(8,128)(2,1)}), bf16[8,2,1,4,128,128]{5,4,3,1,2,0:T(8,128)(2,1)S(1)}, u32[]{:S(2)}, u32[]{:S(2)}) %all-to-all-start.3) | async-done | bytes 2097184 | tf_op jit(solution)/shard_map/all_to_all | solution.py:30
  96.8 2.1 gather_fusion.4
  99.0 7.6 %broadcast_select_fusion.3 = (bf16[16,4,128,128]{3,1,2,0:T(4,128)(2,1)}, bf16[16,4,128,128]{3,1,2,0:T(4,128)(2,1)}, bf16[16,4,128,128]{3,1,2,0:T(4,128)(2,1)}, bf16[16,4,128,128]{3,1,2,0:T(4,128)(2,1)}) fusion(pred[]{:T(512)S(6)} %eq.60, bf16[16,4,128,128]{3,2,1,0:T(8,128)(2,1)} %gather_fusion.4, pred[]{:T(512)S(6)} %eq.63, pred[]{:T(512)S(6)} %eq.67, ...), kind=kLoop, calls=%fused_computation.21 | loop fusion | flops 4194304 | bytes 10485764 | tf_op jit(solution)/shard_map/jit(_where)/select_n | solution.py:42
  106.7 0.7 all-reduce.7.cloned.1.call-update
  107.4 0.9 stack.2
  108.2 4.8 all-to-all-start
  113.1 1.6 scatter_custom_fusion
  116.0 12.2 %all-to-all-done = s32[128,2,8,4]{2,3,1,0:T(4,128)S(1)} async-done(((s32[128,2,8,4]{2,3,1,0:T(4,128)}), s32[128,2,8,4]{2,3,1,0:T(4,128)S(1)}, u32[]{:S(2)}, u32[]{:S(2)}) %all-to-all-start) | async-done | bytes 32800 | tf_op jit(solution)/shard_map/all_to_all | solution.py:71
  128.2 1.0 gather_fusion
  129.2 0.1 dynamic-slice_select_fusion.3
  129.3 0.1 copy.82
  129.4 0.1 copy.83
  129.5 0.1 copy.92
  129.6 0.1 copy.96
  129.7 0.1 copy.91
  129.8 0.1 copy.89
  130.0 0.1 copy.84
  130.0 0.1 copy.97
  130.1 0.1 copy.93
  130.2 129.4 %all-reduce.5.cloned.1.call-done = (bf16[16,4,128,128]{3,1,2,0:T(4,128)(2,1)}, bf16[16,4,128,128]{3,1,2,0:T(4,128)(2,1)}) async-done(((bf16[16,4,128,128]{3,1,2,0:T(4,128)(2,1)}, bf16[16,4,128,128]{3,1,2,0:T(4,128)(2,1)}), (bf16[16,4,128,128]{3,1,2,0:T(4,128)(2,1)}, bf16[16,4,128,128]{3,1,2,0:T(4,128)(2,1)})) %all-reduce.5.cloned.1.call-update) | async-done | bytes 4194320 | tf_op jit(solution)/shard_map/psum | solution.py:42
  259.7 7.1 %convert_bitcast_fusion = bf16[16,128,12,128]{3,2,1,0:T(8,128)(2,1)} fusion(bf16[16,4,128,128]{3,1,2,0:T(4,128)(2,1)} %get-tuple-element.23, s32[16,4]{1,0:T(8,128)S(1)} %copy.97), kind=kOutput, calls=%fused_computation.13 | convolution fusion | flops 28312320 | bytes 8388864 | tf_op jit(solution)/shard_map/nkab,nkj->najb/dot_general | solution.py:57
  266.8 12.2 %copy.99 = bf16[16,128,12,128]{1,3,2,0:T(8,128)(2,1)} copy(bf16[16,128,12,128]{3,2,1,0:T(8,128)(2,1)} %convert_bitcast_fusion) | data formatting | bytes 12582912 | tf_op jit(solution)/shard_map/convert_element_type | solution.py:58
  279.0 6.4 %convert_bitcast_fusion.1 = bf16[16,128,12,128]{3,2,1,0:T(8,128)(2,1)} fusion(bf16[16,4,128,128]{3,1,2,0:T(4,128)(2,1)S(1)} %copy-done.1, s32[16,4]{1,0:T(8,128)S(1)} %copy.93), kind=kOutput, calls=%fused_computation.14 | convolution fusion | flops 28312320 | bytes 8388864 | tf_op jit(solution)/shard_map/nkab,nkj->najb/dot_general | solution.py:57
  285.4 12.0 %copy.95 = bf16[16,128,12,128]{1,3,2,0:T(8,128)(2,1)} copy(bf16[16,128,12,128]{3,2,1,0:T(8,128)(2,1)} %convert_bitcast_fusion.1) | data formatting | bytes 12582912 | tf_op jit(solution)/shard_map/convert_element_type | solution.py:58
  297.4 10.5 %pad_maximum_fusion = bf16[32,128,1536]{1,2,0:T(8,128)(2,1)} fusion(bf16[16,128,1536]{1,2,0:T(8,128)(2,1)} %bitcast.71, bf16[16,128,1536]{1,2,0:T(8,128)(2,1)} %bitcast.72), kind=kLoop, calls=%fused_computation.9 | loop fusion | flops 6291456 | bytes 25165824 | tf_op jit(solution)/shard_map/concatenate | solution.py:112
  307.9 16.7 %copy.100 = bf16[32,128,1536]{2,1,0:T(8,128)(2,1)} copy(bf16[32,128,1536]{1,2,0:T(8,128)(2,1)} %pad_maximum_fusion) | data formatting | bytes 25165824 | tf_op jit(solution)/shard_map/concatenate | solution.py:112
  324.6 120.8 %all-reduce.7.cloned.1.call-done = (bf16[16,4,128,128]{3,1,2,0:T(4,128)(2,1)}, bf16[16,4,128,128]{3,1,2,0:T(4,128)(2,1)}) async-done(((bf16[16,4,128,128]{3,1,2,0:T(4,128)(2,1)}, bf16[16,4,128,128]{3,1,2,0:T(4,128)(2,1)}), (bf16[16,4,128,128]{3,1,2,0:T(4,128)(2,1)}, bf16[16,4,128,128]{3,1,2,0:T(4,128)(2,1)})) %all-reduce.7.cloned.1.call-update) | async-done | bytes 4194320 | tf_op jit(solution)/shard_map/psum | solution.py:42
  445.3 4.0 broadcast_multiply_fusion
  449.4 2.3 broadcast_multiply_fusion.1
  451.7 9.8 %convolution_convert_fusion = bf16[16,32,128,128]{3,1,2,0:T(8,128)(2,1)} fusion(bf16[16,4,128,128]{3,1,2,0:T(4,128)(2,1)} %broadcast_multiply_fusion, bf16[16,4,128,128]{3,1,2,0:T(4,128)(2,1)} %broadcast_multiply_fusion.1, s32[16,8]{1,0:T(8,128)S(1)} %copy.84), kind=kOutput, calls=%fused_computation.12 | convolution fusion | flops 150999040 | bytes 20972032 | tf_op jit(solution)/shard_map/nkab,nkj->najb/dot_general | solution.py:117
  461.6 31.4 %multiply_reduce_fusion = (f32[1536]{0:T(1024)S(1)}, f32[2048,1536]{1,0:T(8,128)}) fusion(bf16[4096,1536]{1,0:T(8,128)(2,1)S(1)} %bitcast.75, bf16[256,8,32,128]{3,2,1,0:T(8,128)(2,1)} %bitcast.70), kind=kOutput, calls=%fused_computation.11 | convolution fusion | flops 25776093184 | bytes 41949184 | tf_op jit(solution)/shard_map/dot_general | solution.py:121
  493.0 14.6 %all_to_all.37 = f32[16,1,1536]{2,1,0:T(1,128)S(1)} all-to-all(f32[16,1,1536]{2,1,0:T(1,128)S(1)} %broadcast_in_dim.48), channel_id=1, replica_groups=mesh['row_0'=4,'row_1'=2,'row_2'=2,'col'=8] {'row_0','row_1','row_2'}, dimensions={0} | all-to-all | bytes 196608 | tf_op jit(solution)/shard_map/all_to_all | solution.py:47
  507.6 0.1 reduce_sum.19
  507.7 9.0 %multiply_convert_fusion = bf16[2048,1536]{1,0:T(8,128)(2,1)} fusion(f32[2048,1536]{1,0:T(8,128)} %get-tuple-element.40, f32[1536]{0:T(1024)S(1)} %add_divide_fusion), kind=kLoop, calls=%fused_computation.10 | loop fusion | flops 9437184 | bytes 18880512 | tf_op jit(solution)/shard_map/convert_element_type | solution.py:126
  (43 shorter events, 0.3 us)
Async XLA Ops:
  9.7 6.5 %copy-start = (s32[256]{0:T(256)S(1)}, s32[256]{0:T(256)}, u32[]{:S(2)}) copy-start(s32[256]{0:T(256)} %param.8) | copy-start | bytes 3076
  9.7 37.1 %all-to-all-start.1 = ((bf16[2,8,4,128,128]{4,3,2,0,1:T(8,128)(2,1)}), bf16[2,8,4,128,128]{4,3,2,0,1:T(8,128)(2,1)S(1)}, u32[]{:S(2)}, u32[]{:S(2)}) async-start(bf16[2,8,4,128,128]{4,3,2,0,1:T(8,128)(2,1)} %copy.85), calls=%async_computation.1 | async-start | bytes 4194304 | tf_op jit(solution)/shard_map/all_to_all | solution.py:81
  58.7 7.2 %copy-start.4 = (s32[2]{0:T(128)S(1)}, s32[2]{0:T(128)}, u32[]{:S(2)}) copy-start(s32[2]{0:T(128)} %param.9) | copy-start | bytes 28
  58.7 38.1 %all-to-all-start.3 = ((bf16[8,2,1,4,128,128]{5,4,3,1,2,0:T(8,128)(2,1)}), bf16[8,2,1,4,128,128]{5,4,3,1,2,0:T(8,128)(2,1)S(1)}, u32[]{:S(2)}, u32[]{:S(2)}) async-start(bf16[8,2,1,4,128,128]{5,4,3,1,2,0:T(8,128)(2,1)} %copy.87), calls=%async_computation.3 | async-start | bytes 4194304 | tf_op jit(solution)/shard_map/all_to_all | solution.py:30
  65.9 193.7 %all-reduce.5.cloned.1.call-start = ((), (), s32[]{:S(2)}) async-start(), calls=%async_computation.5 | async-start | bytes 8388608 | tf_op jit(solution)/shard_map/psum | solution.py:42
  106.6 338.7 %all-reduce.7.cloned.1.call-start = ((), (), s32[]{:S(2)}) async-start(), calls=%async_computation.6 | async-start | bytes 8388608 | tf_op jit(solution)/shard_map/psum | solution.py:42
  106.7 0.7 copy-start.3
  108.2 19.9 %all-to-all-start = ((s32[128,2,8,4]{2,3,1,0:T(4,128)}), s32[128,2,8,4]{2,3,1,0:T(4,128)S(1)}, u32[]{:S(2)}, u32[]{:S(2)}) async-start(s32[128,2,8,4]{2,3,1,0:T(4,128)} %stack.2), calls=%async_computation | async-start | bytes 1048576 | tf_op jit(solution)/shard_map/all_to_all | solution.py:71
  266.8 12.2 %copy-start.1 = (bf16[16,4,128,128]{3,1,2,0:T(4,128)(2,1)S(1)}, bf16[16,4,128,128]{3,1,2,0:T(4,128)(2,1)}, u32[]{:S(2)}) copy-start(bf16[16,4,128,128]{3,1,2,0:T(4,128)(2,1)} %get-tuple-element.24) | copy-start | bytes 6291460
  445.3 4.0 copy-start.2
  449.4 12.2 %slice-start = ((s8[12582912]{0:T(1024)(128)(4,1)}), s8[4194304]{0:T(1024)(128)(4,1)S(1)}, s32[]{:S(2)}) async-start(s8[12582912]{0:T(1024)(128)(4,1)} %bitcast.73), calls=%async_computation.7 | async-start | bytes 8388608
  451.7 9.9 %slice-start.1 = ((s8[12582912]{0:T(1024)(128)(4,1)}), s8[4194304]{0:T(1024)(128)(4,1)S(1)}, s32[]{:S(2)}) async-start(s8[12582912]{0:T(1024)(128)(4,1)} %bitcast.73), calls=%async_computation.8 | async-start | bytes 8388608
  451.7 9.9 %slice-start.2 = ((s8[12582912]{0:T(1024)(128)(4,1)}), s8[4194304]{0:T(1024)(128)(4,1)S(1)}, s32[]{:S(2)}) async-start(s8[12582912]{0:T(1024)(128)(4,1)} %bitcast.73), calls=%async_computation.9 | async-start | bytes 8388608
Sparse Core Ops, SparseCore 0:
  106.7 152.8 all-reduce.4
  262.2 183.0 all-reduce.6
